TPU v7x, 256 devices: a whole 4x4x8 slice. The times are simulated.
256 devices in a mesh: paths: 32 (over x, z_lo, core), trades: 8 (over z_hi, y).
Axes of the slice: x: 4, y: 4, z: 8 (z_hi: 2, z_lo: 4; z = z_hi * 4 + z_lo), core: 2. Of those that a mesh axis runs over, the one named last changes fastest.
Arguments:
- basis: bfloat16 [32768, 512], P('paths'), may hold values from -6 to 6
- coef: bfloat16 [512, 16384], P('paths', 'trades'), may hold values from -0.25 to 0.25
- membership: int32 [16384, 512], P('trades'), may hold values from -1 to 1, as said below
- counts: int32 [512], replicated, may hold values from 1 to 63, as said below
- borrow: float32 [512], replicated, may hold values from 0.3 to 3
- lend: float32 [512], replicated, may hold values from 0.3 to 3
Outputs:
- d_basis: float32 [32768, 512], P(('paths', 'trades'))
- d_coef: float32 [512, 16384], P('paths', 'trades')
Inputs may be any that keep to these rules, and one draw needn't show every extreme that they name: Each row of membership has exactly one nonzero entry, 1 or -1, and every set holds at least one trade. counts[s] is the number of nonzero entries in column s of membership; some set holds exactly one trade and some set exactly 63.
All inputs are finite; a program needn't handle non-finite values.
Results may differ from a plain program's by a relative error of at most 0.0042.
Values may be sent and summed in bfloat16 or wider, within the bound.
No kernel may reach another device: no remote copies, remote signals or barrier semaphores. Data moves between devices by JAX's collectives and lax.ppermute only.
A program may use at most 64 MiB of HBM per device.

v0:
```python
import jax
import jax.numpy as jnp
from jax import lax
from jax.sharding import PartitionSpec as P


def funding(netted, scale, borrow, lend):
    scaled = netted * scale
    grad = (borrow * jax.nn.sigmoid(scaled) + lend * jax.nn.sigmoid(-scaled)) * scale
    return grad.astype(jnp.bfloat16)


def body(basis, coef, membership, counts, borrow, lend):
    path_rows = basis.shape[0]
    member = membership.astype(jnp.bfloat16)
    coef_full = lax.all_gather(coef, "paths", axis=0, tiled=True)
    trade_value = jnp.dot(basis, coef_full, preferred_element_type=jnp.float32)
    exposure = jax.nn.softplus(trade_value).astype(jnp.bfloat16)
    partial_net = jnp.dot(exposure, member, preferred_element_type=jnp.float32)
    scale_all = lax.rsqrt(counts.astype(jnp.float32))
    net_share = lax.psum_scatter(partial_net, "trades", scatter_dimension=1, tiled=True)
    width_sets = net_share.shape[1]
    offset_sets = lax.axis_index("trades") * width_sets
    grad_share = funding(
        net_share,
        lax.dynamic_slice_in_dim(scale_all, offset_sets, width_sets, 0),
        lax.dynamic_slice_in_dim(borrow, offset_sets, width_sets, 0),
        lax.dynamic_slice_in_dim(lend, offset_sets, width_sets, 0),
    )
    set_grad = lax.all_gather(grad_share, "trades", axis=1, tiled=True)
    trade_grad = lax.dot_general(
        set_grad, member, (((1,), (1,)), ((), ())), preferred_element_type=jnp.float32
    )
    value_grad = (trade_grad * jax.nn.sigmoid(trade_value)).astype(jnp.bfloat16)
    d_basis = lax.psum_scatter(
        lax.dot_general(
            value_grad, coef_full, (((1,), (1,)), ((), ())), preferred_element_type=jnp.float32
        ),
        "trades",
        scatter_dimension=0,
        tiled=True,
    )
    factor = 1.0 / jnp.sqrt(jnp.float32(path_rows * lax.axis_size("paths")))
    product = lax.dot_general(
        basis, value_grad, (((0,), (0,)), ((), ())), preferred_element_type=jnp.float32
    )
    d_coef = lax.psum_scatter(product * factor, "paths", scatter_dimension=0, tiled=True)
    return (d_basis, d_coef)


def solution(mesh):
    placed = (P("paths", None), P("paths", "trades"), P("trades", None), P(), P(), P())
    return jax.shard_map(
        body,
        mesh=mesh,
        in_specs=placed,
        out_specs=(P(("paths", "trades"), None), P("paths", "trades")),
        check_vma=False,
    )
```

profile of v0, /device:TPU:16, one launch (start us, length us, event | category | flops | bytes accessed | tf_op | source)
XLA Modules:
  0.0 507.9 jit_solution(12075399827394705610)
XLA Ops:
  7.2 0.0 copy-start
  7.2 0.0 all-gather.3.cloned.1.call-start
  7.2 0.7 all-gather.3.cloned.1.call-update
  7.9 0.0 reduce-scatter.6.cloned.1.call-start
  8.0 64.3 %all-gather.3.cloned.1.call-done = bf16[512,2048]{1,0:T(8,128)(2,1)} async-done(((bf16[16,2048]{1,0:T(8,128)(2,1)}), bf16[512,2048]{1,0:T(8,128)(2,1)}) %all-gather.3.cloned.1.call-update) | async-done | bytes 2097168 | tf_op jit(solution)/shard_map/all_gather | solution.py:16
  72.3 0.0 copy-done
  72.3 0.0 copy-start.2
  72.3 4.1 fusion.6
  76.4 0.0 copy-start.4
  76.4 3.2 copy-done.4
  79.6 0.0 copy-done.2
  79.6 0.0 copy-start.1
  79.6 6.7 %fusion.1 = f32[1024,512]{0,1:T(8,128)} fusion(f32[1024,2048]{1,0:T(8,128)S(1)} %fusion.6, s32[2048,512]{1,0:T(8,128)S(1)} %copy-done.2), kind=kOutput, calls=%fused_computation.4 | convolution fusion | flops 2163212288 | bytes 14680064 | tf_op jit(solution)/shard_map/dot_general | solution.py:19
  86.3 0.0 reduce-scatter.6.cloned.1.call-update
  86.3 0.0 all-gather.5.cloned.1.call-start
  86.4 0.8 dynamic_slice.9
  87.1 0.8 dynamic_slice.11
  87.9 0.0 copy-done.1
  87.9 0.1 dynamic_slice.10
  88.0 91.8 %reduce-scatter.6.cloned.1.call-done = f32[1024,64]{0,1:T(8,128)} async-done(((f32[1024,512]{0,1:T(8,128)}), f32[1024,64]{0,1:T(8,128)}) %reduce-scatter.6.cloned.1.call-update) | async-done | bytes 262160 | tf_op jit(solution)/shard_map/reduce_scatter | solution.py:21
  179.7 1.8 multiply_convert_fusion.1
  181.5 0.0 all-gather.5.cloned.1.call-update
  181.6 0.0 copy-start.3
  181.6 0.0 reduce-scatter.8.cloned.1.call-start
  181.6 58.9 %all-gather.5.cloned.1.call-done = bf16[1024,512]{0,1:T(8,128)(2,1)} async-done(((bf16[1024,64]{0,1:T(8,128)(2,1)}), bf16[1024,512]{0,1:T(8,128)(2,1)}) %all-gather.5.cloned.1.call-update) | async-done | bytes 1048592 | tf_op jit(solution)/shard_map/all_gather | solution.py:30
  240.5 8.5 %multiply_convert_fusion = bf16[1024,2048]{1,0:T(8,128)(2,1)S(1)} fusion(f32[1024,2048]{1,0:T(8,128)} %copy-done.4, bf16[1024,512]{0,1:T(8,128)(2,1)} %all-gather.5.cloned.1.call-done, s32[2048,512]{1,0:T(8,128)} %param.8), kind=kOutput, calls=%fused_computation.2 | convolution fusion | flops 2159017984 | bytes 17825792 | tf_op jit(solution)/shard_map/dot_general | solution.py:31
  249.0 0.0 copy-start.5
  249.1 1.9 copy-done.5
  251.0 0.0 copy-done.3
  251.0 3.7 fusion.7
  254.7 0.0 reduce-scatter.8.cloned.1.call-update
  254.8 0.2 reduce-scatter.10.cloned.1.call-start
  255.0 6.5 %multiply_bitcast_fusion = f32[512,2048]{0,1:T(8,128)} fusion(bf16[1024,2048]{1,0:T(8,128)(2,1)} %copy-done.5, bf16[1024,512]{1,0:T(8,128)(2,1)S(1)} %copy-done), kind=kOutput, calls=%fused_computation.3 | convolution fusion | flops 2148532224 | bytes 9437184 | tf_op jit(solution)/shard_map/dot_general | solution.py:44
  261.5 5.4 %copy.10 = f32[512,2048]{1,0:T(8,128)} copy(f32[512,2048]{0,1:T(8,128)} %multiply_bitcast_fusion) | data formatting | bytes 8388608
  266.9 0.0 reduce-scatter.10.cloned.1.call-update
  267.0 79.4 %reduce-scatter.8.cloned.1.call-done = f32[128,512]{1,0:T(8,128)} async-done(((f32[1024,512]{1,0:T(8,128)}), f32[128,512]{1,0:T(8,128)}) %reduce-scatter.8.cloned.1.call-update) | async-done | bytes 262160 | tf_op jit(solution)/shard_map/reduce_scatter | solution.py:35
  346.3 155.0 %reduce-scatter.10.cloned.1.call-done = f32[16,2048]{1,0:T(8,128)} async-done(((f32[512,2048]{1,0:T(8,128)}), f32[16,2048]{1,0:T(8,128)}) %reduce-scatter.10.cloned.1.call-update) | async-done | bytes 131088
  (1 shorter events, 0.0 us)
Async XLA Ops:
  7.2 65.1 %copy-start = (bf16[1024,512]{1,0:T(8,128)(2,1)S(1)}, bf16[1024,512]{1,0:T(8,128)(2,1)}, u32[]{:S(2)}) copy-start(bf16[1024,512]{1,0:T(8,128)(2,1)} %param.6) | copy-start | bytes 3145732
  7.2 65.1 %all-gather.3.cloned.1.call-start = ((), (), s32[]{:S(2)}) async-start(), calls=%async_computation.3 | async-start | bytes 2162688 | tf_op jit(solution)/shard_map/all_gather | solution.py:16
  7.9 171.8 %reduce-scatter.6.cloned.1.call-start = ((), (), s32[]{:S(2)}) async-start(), calls=%async_computation.4 | async-start | bytes 2359296 | tf_op jit(solution)/shard_map/reduce_scatter | solution.py:21
  72.3 7.3 %copy-start.2 = (s32[2048,512]{1,0:T(8,128)S(1)}, s32[2048,512]{1,0:T(8,128)}, u32[]{:S(2)}) copy-start(s32[2048,512]{1,0:T(8,128)} %param.8) | copy-start | bytes 12582916
  76.4 3.2 copy-start.4
  79.6 8.3 %copy-start.1 = (s32[512]{0:T(512)S(1)}, s32[512]{0:T(512)}, u32[]{:S(2)}) copy-start(s32[512]{0:T(512)} %param.9) | copy-start | bytes 6148
  86.3 154.2 %all-gather.5.cloned.1.call-start = ((), (), s32[]{:S(2)}) async-start(), calls=%async_computation.5 | async-start | bytes 1179648 | tf_op jit(solution)/shard_map/all_gather | solution.py:30
  181.6 69.4 %copy-start.3 = (bf16[512,2048]{1,0:T(8,128)(2,1)S(1)}, bf16[512,2048]{1,0:T(8,128)(2,1)}, u32[]{:S(2)}) copy-start(bf16[512,2048]{1,0:T(8,128)(2,1)} %all-gather.3.cloned.1.call-done) | copy-start | bytes 6291460
  181.6 164.8 %reduce-scatter.8.cloned.1.call-start = ((), (), s32[]{:S(2)}) async-start(), calls=%async_computation.6 | async-start | bytes 2359296 | tf_op jit(solution)/shard_map/reduce_scatter | solution.py:35
  249.0 2.0 copy-start.5
  254.8 246.6 %reduce-scatter.10.cloned.1.call-start = ((), (), s32[]{:S(2)}) async-start(), calls=%async_computation.7 | async-start | bytes 4325376
Sparse Core Ops, SparseCore 0:
  9.8 62.4 all-gather.2
  86.4 93.2 reduce-scatter.5
  182.9 57.5 all-gather.4
  254.9 91.4 reduce-scatter.7
  349.3 152.0 reduce-scatter.9
where the time goes:
time: 508 us
  waiting for transfers between devices  450 us (89%)
  matrix products  29.5 us (6%)
  between operations  13.8 us (3%)
  local copies, waits for them, and re-layouts  12.2 us (2%)
    unnamed x6, waiting for transfers between devices  156 us
    reduce_scatter x1, waiting for transfers between devices, body(): lax.psum_scatter(partial_net, 'trades', scatter_dimension=1, tiled=True)  91.8 us
    reduce_scatter x1, waiting for transfers between devices, body(): lax.psum_scatter(lax.dot_general(value_grad, coef_full, (((1,), (1,)), ((...  79.4 us
    all_gather x1, waiting for transfers between devices, body(): coef_full = lax.all_gather(coef, 'paths', axis=0, tiled=True)  64.3 us
    all_gather x1, waiting for transfers between devices, body(): set_grad = lax.all_gather(grad_share, 'trades', axis=1, tiled=True)  58.9 us
    unnamed x13, local copies, waits for them, and re-layouts  10.6 us
  transfers between devices with their start and end apart: 5, of which 5 were waited for; matrix products, arithmetic and copies ran while one was open for 3% of the time, Pallas kernels for 0%

commit v1 on v0

--- a/solution.py
+++ b/solution.py
@@ -27,7 +27,9 @@
         lax.dynamic_slice_in_dim(borrow, offset_sets, width_sets, 0),
         lax.dynamic_slice_in_dim(lend, offset_sets, width_sets, 0),
     )
-    set_grad = lax.all_gather(grad_share, "trades", axis=1, tiled=True)
+    set_grad = jnp.concatenate(
+        lax.all_to_all(jnp.stack([grad_share] * lax.axis_size("trades")), "trades", 0, 0), axis=1
+    )
     trade_grad = lax.dot_general(
         set_grad, member, (((1,), (1,)), ((), ())), preferred_element_type=jnp.float32
     )

time: 508 us -> 479 us (0.943)
  waiting for transfers between devices: 450 us -> 403 us
  blocking collectives: 0 us -> 19.7 us
    all_gather x1 -> x0, waiting for transfers between devices: 58.9 us -> none  [body(): set_grad = lax.all_gather(grad_share, 'trades', axis=1, tiled=True)]
    all_to_all x0 -> x1, blocking collectives: none -> 19.7 us  [body(): lax.all_to_all(jnp.stack([grad_share] * lax.axis_size('trades')), 'trades...]
    reduce_scatter x1, waiting for transfers between devices: 79.4 us -> 91.1 us  [body(): lax.psum_scatter(lax.dot_general(value_grad, coef_full, (((1,), (1,)), ((...]
    unnamed x6 -> x5, waiting for transfers between devices: 156 us -> 156 us
  transfers between devices with their start and end apart: 5 -> 4, of which waited for: 5 -> 4; matrix products, arithmetic and copies ran while one was open for 3% -> 3% of each run, Pallas kernels for 0% -> 0%
where the time goes in v1:
time: 479 us; the launch traced here: 478 us
  waiting for transfers between devices  403 us (84%)
  matrix products  27.8 us (6%)
  blocking collectives  19.7 us (4%)
  between operations  13.8 us (3%)
  local copies, waits for them, and re-layouts  12.3 us (3%)
    unnamed x5, waiting for transfers between devices  156 us
    reduce_scatter x1, waiting for transfers between devices, body(): lax.psum_scatter(partial_net, 'trades', scatter_dimension=1, tiled=True)  91.8 us
    reduce_scatter x1, waiting for transfers between devices, body(): lax.psum_scatter(lax.dot_general(value_grad, coef_full, (((1,), (1,)), ((...  91.1 us
    all_gather x1, waiting for transfers between devices, body(): coef_full = lax.all_gather(coef, 'paths', axis=0, tiled=True)  64.3 us
    all_to_all x1, blocking collectives, body(): lax.all_to_all(jnp.stack([grad_share] * lax.axis_size('trades')), 'trades...  19.7 us
    unnamed x13, local copies, waits for them, and re-layouts  10.6 us
  transfers between devices with their start and end apart: 4, of which 4 were waited for; matrix products, arithmetic and copies ran while one was open for 3% of the time, Pallas kernels for 0%

profile of v1, /device:TPU:16, one launch (start us, length us, event | category | flops | bytes accessed | tf_op | source)
XLA Modules:
  0.0 477.9 jit_solution(3165041459551390574)
XLA Ops:
  7.2 0.0 copy-start
  7.2 0.0 all-gather.2.cloned.1.call-start
  7.2 0.7 all-gather.2.cloned.1.call-update
  7.9 0.0 reduce-scatter.6.cloned.1.call-start
  8.0 64.3 %all-gather.2.cloned.1.call-done = bf16[512,2048]{1,0:T(8,128)(2,1)} async-done(((bf16[16,2048]{1,0:T(8,128)(2,1)}), bf16[512,2048]{1,0:T(8,128)(2,1)}) %all-gather.2.cloned.1.call-update) | async-done | bytes 2097168 | tf_op jit(solution)/shard_map/all_gather | solution.py:16
  72.3 0.0 copy-done
  72.3 0.0 copy-start.2
  72.3 4.1 fusion.6
  76.4 0.0 copy-start.4
  76.4 3.2 copy-done.4
  79.6 0.0 copy-done.2
  79.6 0.0 copy-start.1
  79.6 6.7 %fusion.1 = f32[1024,512]{0,1:T(8,128)} fusion(f32[1024,2048]{1,0:T(8,128)S(1)} %fusion.6, s32[2048,512]{1,0:T(8,128)S(1)} %copy-done.2), kind=kOutput, calls=%fused_computation.4 | convolution fusion | flops 2163212288 | bytes 14680064 | tf_op jit(solution)/shard_map/dot_general | solution.py:19
  86.3 0.0 reduce-scatter.6.cloned.1.call-update
  86.3 0.0 reduce-scatter.8.cloned.1.call-start
  86.3 0.8 dynamic_slice.9
  87.1 0.8 dynamic_slice.11
  87.9 0.0 copy-done.1
  87.9 0.1 dynamic_slice.10
  87.9 91.8 %reduce-scatter.6.cloned.1.call-done = f32[1024,64]{0,1:T(8,128)} async-done(((f32[1024,512]{0,1:T(8,128)}), f32[1024,64]{0,1:T(8,128)}) %reduce-scatter.6.cloned.1.call-update) | async-done | bytes 262160 | tf_op jit(solution)/shard_map/reduce_scatter | solution.py:21
  179.7 1.2 multiply_convert_fusion.1
  180.9 0.1 stack.2
  181.0 19.7 %all_to_all.5 = bf16[8,1024,64]{1,2,0:T(8,128)(2,1)S(1)} all-to-all(bf16[8,1024,64]{1,2,0:T(8,128)(2,1)S(1)} %stack.2), channel_id=1, replica_groups=mesh['paths'=32,'trades'=8] {'trades'}, dimensions={0} | all-to-all | bytes 2097152 | tf_op jit(solution)/shard_map/all_to_all | solution.py:31
  200.7 0.0 copy-start.3
  200.7 6.9 %multiply_convert_fusion = bf16[1024,2048]{1,0:T(8,128)(2,1)S(1)} fusion(f32[1024,2048]{1,0:T(8,128)} %copy-done.4, bf16[1024,512]{0,1:T(8,128)(2,1)S(1)} %bitcast.13, s32[2048,512]{1,0:T(8,128)} %param.8), kind=kOutput, calls=%fused_computation.2 | convolution fusion | flops 2159017984 | bytes 17825792 | tf_op jit(solution)/shard_map/dot_general | solution.py:33
  207.6 0.0 copy-start.5
  207.6 1.9 copy-done.5
  209.5 0.0 copy-done.3
  209.5 3.7 fusion.7
  213.2 0.0 reduce-scatter.8.cloned.1.call-update
  213.3 0.0 reduce-scatter.10.cloned.1.call-start
  213.3 6.5 %multiply_bitcast_fusion = f32[512,2048]{0,1:T(8,128)} fusion(bf16[1024,2048]{1,0:T(8,128)(2,1)} %copy-done.5, bf16[1024,512]{1,0:T(8,128)(2,1)S(1)} %copy-done), kind=kOutput, calls=%fused_computation.3 | convolution fusion | flops 2148532224 | bytes 9437184 | tf_op jit(solution)/shard_map/dot_general | solution.py:46
  219.9 5.5 %copy.12 = f32[512,2048]{1,0:T(8,128)} copy(f32[512,2048]{0,1:T(8,128)} %multiply_bitcast_fusion) | data formatting | bytes 8388608
  225.3 0.0 reduce-scatter.10.cloned.1.call-update
  225.3 91.1 %reduce-scatter.8.cloned.1.call-done = f32[128,512]{1,0:T(8,128)} async-done(((f32[1024,512]{1,0:T(8,128)}), f32[128,512]{1,0:T(8,128)}) %reduce-scatter.8.cloned.1.call-update) | async-done | bytes 262160 | tf_op jit(solution)/shard_map/reduce_scatter | solution.py:37
  316.5 154.9 %reduce-scatter.10.cloned.1.call-done = f32[16,2048]{1,0:T(8,128)} async-done(((f32[512,2048]{1,0:T(8,128)}), f32[16,2048]{1,0:T(8,128)}) %reduce-scatter.10.cloned.1.call-update) | async-done | bytes 131088
  (1 shorter events, 0.0 us)
Async XLA Ops:
  7.2 65.1 %copy-start = (bf16[1024,512]{1,0:T(8,128)(2,1)S(1)}, bf16[1024,512]{1,0:T(8,128)(2,1)}, u32[]{:S(2)}) copy-start(bf16[1024,512]{1,0:T(8,128)(2,1)} %param.6) | copy-start | bytes 3145732
  7.2 65.1 %all-gather.2.cloned.1.call-start = ((), (), s32[]{:S(2)}) async-start(), calls=%async_computation.4 | async-start | bytes 2162688 | tf_op jit(solution)/shard_map/all_gather | solution.py:16
  7.9 171.8 %reduce-scatter.6.cloned.1.call-start = ((), (), s32[]{:S(2)}) async-start(), calls=%async_computation.5 | async-start | bytes 2359296 | tf_op jit(solution)/shard_map/reduce_scatter | solution.py:21
  72.3 7.3 %copy-start.2 = (s32[2048,512]{1,0:T(8,128)S(1)}, s32[2048,512]{1,0:T(8,128)}, u32[]{:S(2)}) copy-start(s32[2048,512]{1,0:T(8,128)} %param.8) | copy-start | bytes 12582916
  76.4 3.2 copy-start.4
  79.6 8.2 %copy-start.1 = (s32[512]{0:T(512)S(1)}, s32[512]{0:T(512)}, u32[]{:S(2)}) copy-start(s32[512]{0:T(512)} %param.9) | copy-start | bytes 6148
  86.3 230.2 %reduce-scatter.8.cloned.1.call-start = ((), (), s32[]{:S(2)}) async-start(), calls=%async_computation.6 | async-start | bytes 2359296 | tf_op jit(solution)/shard_map/reduce_scatter | solution.py:37
  200.7 8.8 %copy-start.3 = (bf16[512,2048]{1,0:T(8,128)(2,1)S(1)}, bf16[512,2048]{1,0:T(8,128)(2,1)}, u32[]{:S(2)}) copy-start(bf16[512,2048]{1,0:T(8,128)(2,1)} %all-gather.2.cloned.1.call-done) | copy-start | bytes 6291460
  207.6 1.9 copy-start.5
  213.3 258.1 %reduce-scatter.10.cloned.1.call-start = ((), (), s32[]{:S(2)}) async-start(), calls=%async_computation.7 | async-start | bytes 4325376
Sparse Core Ops, SparseCore 0:
  9.8 62.4 all-gather.1
  86.4 93.2 reduce-scatter.5
  213.4 103.0 reduce-scatter.7
  319.4 151.8 reduce-scatter.9
